TPU v7x, 256 devices: a whole 4x4x8 slice. The times are simulated.
256 devices in a mesh: section: 16 (over x_lo, y, core), batch: 16 (over x_hi, z).
Axes of the slice: x: 4 (x_hi: 2, x_lo: 2; x = x_hi * 2 + x_lo), y: 4, z: 8, core: 2. Of those that a mesh axis runs over, the one named last changes fastest.
Arguments:
- states: bfloat16 [32, 32, 64, 1024], P('section', 'batch'), may hold values from -6 to 6
- weights: bfloat16 [32, 64, 576], P('section'), may hold values from -0.25 to 0.25
- guess: float32 [16, 32, 64, 1024], P('section', 'batch'), may hold values from -6 to 6
- loss_cotangent: float32 [32, 64, 1024], P('batch'), may hold values from -6 to 6
Outputs:
- start_cotangents: float32 [16, 32, 64, 1024], P('section', 'batch')
- weight_grads: float32 [32, 36864], P('section', 'batch')
All inputs are finite; a program needn't handle non-finite values.
Results may differ from a plain program's by a relative error of at most 0.0039.
Values may be sent and summed in bfloat16 or wider, within the bound.
No kernel may reach another device: no remote copies, remote signals or barrier semaphores. Data moves between devices by JAX's collectives and lax.ppermute only.
A program may use at most 128 MiB of HBM per device.

v0:
```python
import jax
import jax.numpy as jnp
from jax import lax
from jax.experimental import pallas as pl
from jax.experimental.pallas import tpu as pltpu
from jax.sharding import PartitionSpec as P


H = 0.0625
SIDE = 32
C = 64
N = SIDE * SIDE
LANES = 128
F32 = jnp.float32
BF16 = jnp.bfloat16
WIDE = 640
LEAD = 2 * N + 18 * C


def masked(values, keep):
    return jnp.where(keep, values, jnp.zeros_like(values))


def lane(shape):
    return lax.broadcasted_iota(jnp.int32, shape, len(shape) - 1)


def cols3(v):
    v = v.astype(BF16)
    column = lane(v.shape) & (SIDE - 1)
    ahead = masked(pltpu.roll(v, N - 1, 1), column < SIDE - 1)
    behind = masked(pltpu.roll(v, 1, 1), column > 0)
    return jnp.concatenate([ahead, v, behind], axis=0)


def row_up(t):
    t = pltpu.roll(t, SIDE, 1)
    edge = t[:, :LANES]
    return jnp.concatenate([masked(edge, lane(edge.shape) >= SIDE), t[:, LANES:]], axis=1)


def row_down(t):
    t = pltpu.roll(t, N - SIDE, 1)
    edge = t[:, N - LANES :]
    return jnp.concatenate([t[:, : N - LANES], masked(edge, lane(edge.shape) < LANES - SIDE)], axis=1)


def rows3(t):
    t = t.astype(BF16)
    return jnp.concatenate([row_up(t), t, row_down(t)], axis=0)


def taps(w):
    blocks = [
        jnp.concatenate([w[:, (3 * a + b) * C : (3 * a + b + 1) * C] for a in range(3)], axis=1)
        for b in range(3)
    ]
    return jnp.concatenate(blocks, axis=0).astype(F32).T.astype(BF16)


def conv(m, x3):
    y = jnp.dot(m, x3, preferred_element_type=F32)
    low = row_down(y[:C].astype(BF16))
    high = row_up(y[2 * C :].astype(BF16))
    return y[C : 2 * C] + low.astype(F32) + high.astype(F32)


def flatten_taps(m):
    wide = [m[a * C : (a + 1) * C, : 2 * C] for a in range(3)]
    thin = [m[a * C : (a + 1) * C, 2 * C :] for a in range(3)]
    return jnp.concatenate(wide + thin, axis=1)


def pair_taps(even, odd):
    thin = [flat[:, (6 + a) * C : (7 + a) * C] for a in range(3) for flat in (even, odd)]
    return jnp.concatenate([even[:, : 6 * C], odd[:, : 6 * C]] + thin, axis=1)


def one_of_pair(pair, which):
    wide = [pair[:, (6 * which + 2 * a) * C : (6 * which + 2 * a + 2) * C] for a in range(3)]
    thin = [pair[:, (12 + 2 * a + which) * C : (13 + 2 * a + which) * C] for a in range(3)]
    return jnp.concatenate([jnp.concatenate(wide, axis=0), jnp.concatenate(thin, axis=0)], axis=1)


def core():
    return lax.rem(lax.axis_index("section"), 2)


def moves(pairs, sems, first=0):
    made = [pltpu.make_async_copy(a, b, sems.at[first + n]) for n, (a, b) in enumerate(pairs)]
    for one in made:
        one.start()
    return made


def settle(made):
    for one in made:
        one.wait()


def part_of(u, g, lc, m0, m1):
    t1 = jnp.tanh(u[1].astype(F32))
    t0 = jnp.tanh(u[0].astype(F32))
    d0 = H - H * (t0 * t0)
    t = (H - H * (t1 * t1)) * conv(m1, cols3(g))
    p = t + d0 * conv(m0, cols3(t - g + 2.0 * lc))
    return (2.0 * d0).astype(BF16), p.astype(BF16)


def source_kernel(states, weights, guess, loss, give, keep, ms, u, w, g, lc, sems):
    own = core()
    in_w, *ins = moves([(weights, w), (states, u), (guess.at[0], g), (loss, lc)], sems)
    in_w.wait()
    m1, m0 = taps(w[1]), taps(w[0])
    ms[0], ms[1] = m0, m1
    give[:, 2 * N : 2 * N + 9 * C] = flatten_taps(m0)
    give[:, 2 * N + 9 * C :] = jnp.zeros((C, WIDE - 9 * C), BF16)
    settle(ins)
    for i, out in ((1 - own, give), (own, keep)):
        out[:, :N], out[:, N : 2 * N] = part_of(u.at[:, i], g[i], lc[i], m0, m1)


def merge_kernel(keep, got, ms, out, odd):
    even = core() == 0
    mine, theirs = flatten_taps(ms[0]), got[:, 2 * N : 2 * N + 9 * C]
    both = pair_taps(jnp.where(even, mine, theirs), jnp.where(even, theirs, mine))
    d_even = jnp.where(even, keep[:, :N], got[:, :N])
    d_odd = jnp.where(even, got[:, :N], keep[:, :N])
    p_even = jnp.where(even, keep[:, N:], got[:, N : 2 * N])
    p_odd = jnp.where(even, got[:, N : 2 * N], keep[:, N:])
    odd[...] = p_odd
    y = conv(one_of_pair(both, 0), cols3(p_odd))
    merged = (p_even.astype(F32) + p_odd.astype(F32) + d_even.astype(F32) * y).astype(BF16)
    for k in range(out.shape[0]):
        out[k, :, :N] = d_even
        out[k, :, N : 2 * N] = d_odd
        out[k, :, 2 * N : LEAD] = both
        out[k, :, LEAD:] = merged


def prep_kernel(states, loss, acts, slopes, base):
    base[...] = loss[core()]
    for layer in range(2):
        for i in range(2):
            t = jnp.tanh(states[layer, i].astype(F32))
            acts[layer, i] = rows3(t)
            slopes[layer, i] = H - H * (t * t)


def apply(packed, k, which, e):
    m = one_of_pair(packed[k, :, 2 * N : LEAD], which)
    return e + packed[k, :, which * N : (which + 1) * N].astype(F32) * conv(m, cols3(e))


def upper_kernel(packed, last):
    chips = packed.shape[0]

    def step(r, e):
        k = chips - 1 - r
        x = apply(packed, k, 1, e)
        return apply(packed, k, 0, x) + packed[k, :, LEAD:].astype(F32)

    e = packed[chips - 1, :, LEAD:].astype(F32)
    last[...] = lax.fori_loop(1, chips, step, e).astype(BF16)


def lower_kernel(start, packed, odd, base, mine, other, high, low):
    chips = packed.shape[0]
    spot = lax.rem(lax.axis_index("section") // 2, chips)

    def step(r, e):
        k = chips - 1 - r
        x = apply(packed, k, 1, e)

        @pl.when(k == spot)
        def _():
            high[...] = e
            low[...] = x

        return apply(packed, k, 0, x) + packed[k, :, LEAD:].astype(F32)

    e = lax.fori_loop(0, chips - 1, step, start[...].astype(F32))
    x = apply(packed, 0, 1, e)

    @pl.when(spot == 0)
    def _():
        high[...] = e
        low[...] = x

    at_high = high[...] + base[...]
    at_low = low[...] + odd[...].astype(F32) + base[...]
    even = core() == 0
    mine[...] = jnp.where(even, at_low, at_high)
    other[...] = jnp.where(even, at_high, at_low)


def finish(i, ms, acts, slopes, v):
    x3 = cols3(v)
    first = lax.dot_general(x3, acts[1, i], (((1,), (1,)), ((), ())), preferred_element_type=F32)
    x3 = cols3(v + slopes[1, i] * conv(ms[1], x3))
    return lax.dot_general(x3, acts[0, i], (((1,), (1,)), ((), ())), preferred_element_type=F32), first


def own_kernel(ms, acts, slopes, mine, sums):
    sums[0], sums[1] = finish(core(), ms, acts, slopes, mine[...])


def other_kernel(ms, acts, slopes, other, sums, grads):
    products = finish(1 - core(), ms, acts, slopes, other[...])
    parts = grads.shape[0]
    rows = C // parts
    wides = []
    for layer in range(2):
        g = (sums[layer] + products[layer]) * H
        wides.append(jnp.concatenate(
            [g[b * C : (b + 1) * C, a * C : (a + 1) * C] for a in range(3) for b in range(3)], axis=1
        ))
    for d in range(parts):
        both = [wide[d * rows : (d + 1) * rows] for wide in wides]
        grads[d] = jnp.concatenate(both, axis=0).astype(grads.dtype)


def start_kernel(ms, slopes, mine, theirs, starts):
    for i, lam in ((core(), mine), (1 - core(), theirs)):
        v = lam[...]
        for layer in (1, 0):
            v = v + slopes[layer, i] * conv(ms[layer], cols3(v))
        starts[0, i] = v


def total_kernel(parts, out):
    rows = parts.shape[1] // 2
    s = parts[0].astype(F32)
    for d in range(1, parts.shape[0]):
        s = s + parts[d].astype(F32)
    for layer in range(2):
        out[layer : layer + 1, :] = jnp.concatenate(
            [s[layer * rows + r : layer * rows + r + 1] for r in range(rows)], axis=1
        )


def call(kernel, outs, where_in, where_out, scratch, n_sems, flops, moved, grant=16 << 20):
    spaces = {"s": pltpu.SMEM, "v": pltpu.VMEM, "h": pltpu.HBM}
    specs = lambda text: [pl.BlockSpec(memory_space=spaces[k]) for k in text]
    out_specs = specs(where_out)
    return pl.pallas_call(
        kernel,
        out_shape=outs,
        in_specs=specs(where_in),
        out_specs=tuple(out_specs) if isinstance(outs, tuple) else out_specs[0],
        scratch_shapes=[pltpu.VMEM(*one) for one in scratch]
        + ([pltpu.SemaphoreType.DMA((n_sems,))] if n_sems else []),
        cost_estimate=pl.CostEstimate(flops=flops, bytes_accessed=moved, transcendentals=0),
        compiler_params=pltpu.CompilerParams(vmem_limit_bytes=grant),
    )


def shards(states, weights, guess, loss):
    sections = lax.axis_size("section")
    nb = lax.axis_size("batch")
    half = sections // 2
    chips = half // 2
    shape = jax.ShapeDtypeStruct
    image, image16 = shape((C, N), F32), shape((C, N), BF16)

    swap = [(i, i ^ 1) for i in range(sections)]
    give, keep, ms = call(
        source_kernel,
        (shape((C, 2 * N + WIDE), BF16), shape((C, 2 * N), BF16), shape((2, 3 * C, 3 * C), BF16)), "hhhh", "vvv",
        [((2, 2, C, N), BF16), ((2, C, 9 * C), BF16), ((2, C, N), F32), ((2, C, N), F32)],
        4, 6 * 10**8, 2 * 10**6,
    )(*[pltpu.with_memory_space_constraint(x, pltpu.HBM) for x in (states, weights, guess, loss)])
    got = lax.ppermute(give, "section", swap)
    pairs, odd = call(
        merge_kernel, (shape((chips, C, LEAD + N), BF16), image16), "vvv", "vv", [], 0, 10**8, 3 * 10**6,
    )(keep, got, ms)
    groups = [[x * half + 2 * y + c for y in range(chips)] for x in range(2) for c in range(2)]
    packed = lax.all_to_all(pairs, "section", 0, 0, axis_index_groups=groups, tiled=True)
    acts, slopes, base = call(
        prep_kernel, (shape((2, 2, 3 * C, N), BF16), shape((2, 2, C, N), F32), image),
        "vv", "vvv", [], 0, 10**8, 4 * 10**6,
    )(states, loss)

    last = call(upper_kernel, image16, "v", "v", [], 0, 10**9, 2 * 10**6)(packed)
    carried = lax.ppermute(last, "section", [(i, i - half) for i in range(half, sections)])
    mine, other = call(
        lower_kernel, (image, image), "vvvv", "vv",
        [((C, N), F32), ((C, N), F32)], 0, 12 * 10**8, 2 * 10**6
    )(carried, packed, odd, base)
    theirs = lax.ppermute(other, "section", swap)

    sums = call(own_kernel, shape((2, 3 * C, 3 * C), F32), "vvvv", "v", [], 0, 4 * 10**8, 10**6)(ms, acts, slopes, mine)
    grads = call(
        other_kernel, shape((nb, 2 * (C // nb), 9 * C), BF16), "vvvvv", "v", [], 0, 4 * 10**8, 10**6
    )(ms, acts, slopes, theirs, sums)
    starts = call(start_kernel, shape((1, 2, C, N), F32), "vvvv", "v", [], 0, 6 * 10**8, 3 * 10**6)(
        ms, slopes, mine, theirs
    )
    grads = lax.all_to_all(grads, "batch", 0, 0, tiled=True)
    total = call(total_kernel, shape((2, 9 * C * C // nb), F32), "v", "v", [], 0, 10**6, 10**6)(grads)
    return starts, total


def solution(mesh):
    placed = (
        P("section", "batch", None, None),
        P("section", None, None),
        P("section", "batch", None, None),
        P("batch", None, None),
    )
    return jax.shard_map(
        shards,
        mesh=mesh,
        in_specs=placed,
        out_specs=(P("section", "batch", None, None), P("section", "batch")),
        check_vma=False,
    )
```

profile of v0, /device:TPU:32, one launch (start us, length us, event | category | flops | bytes accessed | tf_op | source)
XLA Modules:
  0.0 75.5 jit_solution(9524643291915535068)
XLA Ops:
  0.6 2.9 %shard_map.59 = (bf16[64,2688]{1,0:T(8,128)(2,1)S(1)}, bf16[64,2048]{1,0:T(8,128)(2,1)S(1)}, bf16[2,192,192]{2,1,0:T(8,128)(2,1)S(1)}) custom-call(bf16[2,2,64,1024]{3,2,1,0:T(8,128)(2,1)} %states.3, bf16[2,64,576]{2,1,0:T(8,128)(2,1)} %weights.1, f32[1,2,64,1024]{3,2,1,0:T(8,128)} %guess.1, f32[2,64,1024]{2,1,0:T(8,128)} %loss.3), custom_call_target="tpu_custom_call" | custom-call | flops 600000000 | bytes 2000000 | tf_op jit(solution)/shard_map/pallas_call | solution.py:267
  3.5 0.1 collective-permute-start
  3.6 1.6 %collective-permute-done.got = bf16[64,2688]{1,0:T(8,128)(2,1)S(1)} collective-permute-done((bf16[64,2688]{1,0:T(8,128)(2,1)S(1)}, bf16[64,2688]{1,0:T(8,128)(2,1)S(1)}, u32[]{:S(2)}, u32[]{:S(2)}) %collective-permute-start) | collective-permute-done | bytes 344096 | tf_op jit(solution)/shard_map/ppermute | solution.py:273
  5.2 0.5 shard_map.61
  5.8 31.6 %all_to_all.10.packed = bf16[4,64,4224]{2,1,0:T(8,128)(2,1)S(1)} all-to-all(bf16[4,64,4224]{2,1,0:T(8,128)(2,1)S(1)} %get-tuple-element.16), channel_id=1, replica_groups={{0,32,64,96},{16,48,80,112},{128,160,192,224},{144,176,208,240},{1,33,6..., dimensions={0} | all-to-all | bytes 4325376 | tf_op jit(solution)/shard_map/all_to_all | solution.py:278
  37.4 0.0 copy-start
  37.4 0.0 copy-start.1
  37.4 2.6 %shard_map.62 = bf16[64,1024]{1,0:T(8,128)(2,1)S(1)} custom-call(bf16[4,64,4224]{2,1,0:T(8,128)(2,1)S(1)} %all_to_all.10.packed), custom_call_target="tpu_custom_call" | custom-call | flops 1000000000 | bytes 2000000 | tf_op jit(solution)/shard_map/pallas_call | solution.py:284
  40.0 1.3 %collective-permute-start.1 = (bf16[64,1024]{1,0:T(8,128)(2,1)S(1)}, bf16[64,1024]{1,0:T(8,128)(2,1)S(1)}, u32[]{:S(2)}, u32[]{:S(2)}) collective-permute-start(bf16[64,1024]{1,0:T(8,128)(2,1)S(1)} %shard_map.62), channel_id=1, source_target_pairs={{128,0},{144,16},{160,32},{176,48},{192,64},{208,80},{224,96},{240... | collective-permute-start | bytes 393224 | tf_op jit(solution)/shard_map/ppermute | solution.py:285
  41.3 0.0 copy-done
  41.3 0.0 copy-done.1
  41.3 0.4 shard_map.60
  41.7 5.1 %collective-permute-done.1.start = bf16[64,1024]{1,0:T(8,128)(2,1)S(1)} collective-permute-done((bf16[64,1024]{1,0:T(8,128)(2,1)S(1)}, bf16[64,1024]{1,0:T(8,128)(2,1)S(1)}, u32[]{:S(2)}, u32[]{:S(2)}) %collective-permute-start.1) | collective-permute-done | bytes 131104 | tf_op jit(solution)/shard_map/ppermute | solution.py:285
  46.9 3.2 %shard_map.63 = (f32[64,1024]{1,0:T(8,128)S(1)}, f32[64,1024]{1,0:T(8,128)S(1)}) custom-call(bf16[64,1024]{1,0:T(8,128)(2,1)S(1)} %collective-permute-done.1.start, bf16[4,64,4224]{2,1,0:T(8,128)(2,1)S(1)} %all_to_all.10.packed, bf16[64,1024]{1,0:T(8,128)(2,1)S(1)} %get-tuple-element.17.odd, f32[64,1024]{1,0:T(8,128)S(1)} %get-tuple-element.18.base), custom_call_target="tpu_custom_call" | custom-call | flops 1200000000 | bytes 2000000 | tf_op jit(solution)/shard_map/pallas_call | solution.py:286
  50.1 0.1 collective-permute-start.2
  50.2 0.9 %shard_map.65.sums = f32[2,192,192]{2,1,0:T(8,128)S(1)} custom-call(bf16[2,192,192]{2,1,0:T(8,128)(2,1)S(1)} %get-tuple-element.12.ms, bf16[2,2,192,1024]{3,2,1,0:T(8,128)(2,1)S(1)} %get-tuple-element.21.acts, f32[2,2,64,1024]{3,2,1,0:T(8,128)S(1)} %get-tuple-element.13.slopes, f32[64,1024]{1,0:T(8,128)S(1)} %get-tuple-element.19.mine), custom_call_target="tpu_custom_call" | custom-call | flops 400000000 | bytes 1000000 | tf_op jit(solution)/shard_map/pallas_call | solution.py:292
  51.2 0.6 collective-permute-done.2.theirs.other
  51.7 1.7 %shard_map.66 = bf16[16,8,576]{2,1,0:T(8,128)(2,1)} custom-call(bf16[2,192,192]{2,1,0:T(8,128)(2,1)S(1)} %get-tuple-element.12.ms, bf16[2,2,192,1024]{3,2,1,0:T(8,128)(2,1)S(1)} %get-tuple-element.21.acts, f32[2,2,64,1024]{3,2,1,0:T(8,128)S(1)} %get-tuple-element.13.slopes, f32[64,1024]{1,0:T(8,128)S(1)} %collective-permute-done.2.theirs.other, ...), custom_call_target="tpu_custom_call" | custom-call | flops 400000000 | bytes 1000000 | tf_op jit(solution)/shard_map/pallas_call | solution.py:293
  53.4 11.0 %all-to-all-start.1 = ((bf16[16,8,576]{2,1,0:T(8,128)(2,1)}), bf16[16,8,576]{2,1,0:T(8,128)(2,1)S(1)}, u32[]{:S(2)}, u32[]{:S(2)}) async-start(bf16[16,8,576]{2,1,0:T(8,128)(2,1)} %shard_map.66), calls=%async_computation.1 | async-start | bytes 327680 | tf_op jit(solution)/shard_map/all_to_all | solution.py:299
  64.4 2.1 %shard_map.64 = f32[1,2,64,1024]{3,2,1,0:T(8,128)} custom-call(bf16[2,192,192]{2,1,0:T(8,128)(2,1)S(1)} %get-tuple-element.12.ms, f32[2,2,64,1024]{3,2,1,0:T(8,128)S(1)} %get-tuple-element.13.slopes, f32[64,1024]{1,0:T(8,128)S(1)} %get-tuple-element.19.mine, f32[64,1024]{1,0:T(8,128)S(1)} %collective-permute-done.2.theirs.other), custom_call_target="tpu_custom_call" | custom-call | flops 600000000 | bytes 3000000 | tf_op jit(solution)/shard_map/pallas_call | solution.py:296
  66.6 8.2 %all-to-all-done.1.parts = bf16[16,8,576]{2,1,0:T(8,128)(2,1)S(1)} async-done(((bf16[16,8,576]{2,1,0:T(8,128)(2,1)}), bf16[16,8,576]{2,1,0:T(8,128)(2,1)S(1)}, u32[]{:S(2)}, u32[]{:S(2)}) %all-to-all-start.1) | async-done | bytes 147488 | tf_op jit(solution)/shard_map/all_to_all | solution.py:299
  74.8 0.7 shard_map.67
Async XLA Ops:
  3.5 1.7 %collective-permute-start = (bf16[64,2688]{1,0:T(8,128)(2,1)S(1)}, bf16[64,2688]{1,0:T(8,128)(2,1)S(1)}, u32[]{:S(2)}, u32[]{:S(2)}) collective-permute-start(bf16[64,2688]{1,0:T(8,128)(2,1)S(1)} %get-tuple-element.15), channel_id=1, source_target_pairs={{0,16},{16,0},{32,48},{48,32},{64,80},{80,64},{96,112},{112,96},{1... | collective-permute-start | bytes 1032200 | tf_op jit(solution)/shard_map/ppermute | solution.py:273
  37.4 3.9 %copy-start = (bf16[2,2,64,1024]{3,2,1,0:T(8,128)(2,1)S(1)}, bf16[2,2,64,1024]{3,2,1,0:T(8,128)(2,1)}, u32[]{:S(2)}) copy-start(bf16[2,2,64,1024]{3,2,1,0:T(8,128)(2,1)} %states.3) | copy-start | bytes 1572868
  37.4 3.9 %copy-start.1 = (f32[2,64,1024]{2,1,0:T(8,128)S(1)}, f32[2,64,1024]{2,1,0:T(8,128)}, u32[]{:S(2)}) copy-start(f32[2,64,1024]{2,1,0:T(8,128)} %loss.3) | copy-start | bytes 1572868
  40.0 6.9 %collective-permute-start.1 = (bf16[64,1024]{1,0:T(8,128)(2,1)S(1)}, bf16[64,1024]{1,0:T(8,128)(2,1)S(1)}, u32[]{:S(2)}, u32[]{:S(2)}) collective-permute-start(bf16[64,1024]{1,0:T(8,128)(2,1)S(1)} %shard_map.62), channel_id=1, source_target_pairs={{128,0},{144,16},{160,32},{176,48},{192,64},{208,80},{224,96},{240... | collective-permute-start | bytes 393224 | tf_op jit(solution)/shard_map/ppermute | solution.py:285
  50.1 1.6 %collective-permute-start.2 = (f32[64,1024]{1,0:T(8,128)S(1)}, f32[64,1024]{1,0:T(8,128)S(1)}, u32[]{:S(2)}, u32[]{:S(2)}) collective-permute-start(f32[64,1024]{1,0:T(8,128)S(1)} %get-tuple-element.20), channel_id=1, source_target_pairs={{0,16},{16,0},{32,48},{48,32},{64,80},{80,64},{96,112},{112,96},{1... | collective-permute-start | bytes 786440 | tf_op jit(solution)/shard_map/ppermute | solution.py:290
  53.4 21.4 %all-to-all-start.1 = ((bf16[16,8,576]{2,1,0:T(8,128)(2,1)}), bf16[16,8,576]{2,1,0:T(8,128)(2,1)S(1)}, u32[]{:S(2)}, u32[]{:S(2)}) async-start(bf16[16,8,576]{2,1,0:T(8,128)(2,1)} %shard_map.66), calls=%async_computation.1 | async-start | bytes 327680 | tf_op jit(solution)/shard_map/all_to_all | solution.py:299
where the time goes:
time: 75.8 us; the launch traced here: 75.5 us
  blocking collectives  31.6 us (42%)
  waiting for transfers between devices  15.6 us (21%)
  Pallas kernels  15.1 us (20%)
  starting transfers between devices  12.5 us (16%)
    all_to_all x1, blocking collectives, shards(): lax.all_to_all(pairs, 'section', 0, 0, axis_index_groups=groups, tiled=True)  31.6 us
    all_to_all x1, starting transfers between devices, shards(): grads = lax.all_to_all(grads, 'batch', 0, 0, tiled=True)  11 us
    all_to_all x1, waiting for transfers between devices, shards(): grads = lax.all_to_all(grads, 'batch', 0, 0, tiled=True)  8.23 us
    ppermute x1, waiting for transfers between devices, shards(): lax.ppermute(last, 'section', [(i, i - half) for i in range(half, section...  5.13 us
    pallas_call x1, Pallas kernels, shards(): call(lower_kernel, (image, image), 'vvvv', 'vv', [((C, N), F32), ((C, N),...  3.24 us
    pallas_call x1, Pallas kernels, shards(): call(source_kernel, (shape((C, 2 * N + WIDE), BF16), shape((C, 2 * N), BF...  2.86 us
    pallas_call x1, Pallas kernels, shards(): call(upper_kernel, image16, 'v', 'v', [], 0, 10 ** 9, 2 * 10 ** 6)(packed)  2.62 us
    pallas_call x1, Pallas kernels, shards(): call(start_kernel, shape((1, 2, C, N), F32), 'vvvv', 'v', [], 0, 6 * 10 *...  2.14 us
  transfers between devices with their start and end apart: 4, of which 4 were waited for; matrix products, arithmetic and copies ran while one was open for 0% of the time, Pallas kernels for 5%

commit v1 on v0

--- a/solution.py
+++ b/solution.py
@@ -107,17 +107,30 @@
     return (2.0 * d0).astype(BF16), p.astype(BF16)
 
 
-def source_kernel(states, weights, guess, loss, give, keep, ms, u, w, g, lc, sems):
+def give_kernel(states, weights, guess, loss, give, ms, u, g, lc, w, u_give, g_give, lc_give, sems):
     own = core()
-    in_w, *ins = moves([(weights, w), (states, u), (guess.at[0], g), (loss, lc)], sems)
+    other = 1 - own
+    in_w, *first = moves(
+        [(weights, w), (states.at[0, other], u_give.at[0]), (states.at[1, other], u_give.at[1]),
+         (guess.at[0, other], g_give), (loss.at[other], lc_give)],
+        sems,
+    )
+    second = moves(
+        [(states.at[0, own], u.at[0]), (states.at[1, own], u.at[1]), (guess.at[0, own], g), (loss.at[own], lc)],
+        sems, 5,
+    )
     in_w.wait()
     m1, m0 = taps(w[1]), taps(w[0])
     ms[0], ms[1] = m0, m1
     give[:, 2 * N : 2 * N + 9 * C] = flatten_taps(m0)
     give[:, 2 * N + 9 * C :] = jnp.zeros((C, WIDE - 9 * C), BF16)
-    settle(ins)
-    for i, out in ((1 - own, give), (own, keep)):
-        out[:, :N], out[:, N : 2 * N] = part_of(u.at[:, i], g[i], lc[i], m0, m1)
+    settle(first)
+    give[:, :N], give[:, N : 2 * N] = part_of(u_give, g_give[...], lc_give[...], m0, m1)
+    settle(second)
+
+
+def keep_kernel(ms, u, g, lc, keep):
+    keep[:, :N], keep[:, N:] = part_of(u, g[...], lc[...], ms[0], ms[1])
 
 
 def merge_kernel(keep, got, ms, out, odd):
@@ -209,15 +222,15 @@
     products = finish(1 - core(), ms, acts, slopes, other[...])
     parts = grads.shape[0]
     rows = C // parts
-    wides = []
-    for layer in range(2):
-        g = (sums[layer] + products[layer]) * H
-        wides.append(jnp.concatenate(
-            [g[b * C : (b + 1) * C, a * C : (a + 1) * C] for a in range(3) for b in range(3)], axis=1
-        ))
+    g = [(sums[layer] + products[layer]) * H for layer in range(2)]
+    cut = 2 * C
+    rest = jnp.concatenate([g[0][:, cut:], g[1][:, cut:]], axis=1)
     for d in range(parts):
-        both = [wide[d * rows : (d + 1) * rows] for wide in wides]
-        grads[d] = jnp.concatenate(both, axis=0).astype(grads.dtype)
+        pieces = [
+            piece[b * C + d * rows : b * C + (d + 1) * rows]
+            for piece in (g[0][:, :cut], g[1][:, :cut], rest) for b in range(3)
+        ]
+        grads[d] = jnp.concatenate(pieces, axis=0).astype(grads.dtype)
 
 
 def start_kernel(ms, slopes, mine, theirs, starts):
@@ -229,14 +242,18 @@
 
 
 def total_kernel(parts, out):
-    rows = parts.shape[1] // 2
+    rows = parts.shape[1] // 9
     s = parts[0].astype(F32)
     for d in range(1, parts.shape[0]):
         s = s + parts[d].astype(F32)
+
+    def tap(layer, a, b):
+        block, start = (2, layer * C) if a == 2 else (layer, a * C)
+        return s[(3 * block + b) * rows : (3 * block + b + 1) * rows, start : start + C]
+
     for layer in range(2):
-        out[layer : layer + 1, :] = jnp.concatenate(
-            [s[layer * rows + r : layer * rows + r + 1] for r in range(rows)], axis=1
-        )
+        wide = jnp.concatenate([tap(layer, a, b) for a in range(3) for b in range(3)], axis=1)
+        out[layer : layer + 1, :] = jnp.concatenate([wide[r : r + 1] for r in range(rows)], axis=1)
 
 
 def call(kernel, outs, where_in, where_out, scratch, n_sems, flops, moved, grant=16 << 20):
@@ -264,13 +281,14 @@
     image, image16 = shape((C, N), F32), shape((C, N), BF16)
 
     swap = [(i, i ^ 1) for i in range(sections)]
-    give, keep, ms = call(
-        source_kernel,
-        (shape((C, 2 * N + WIDE), BF16), shape((C, 2 * N), BF16), shape((2, 3 * C, 3 * C), BF16)), "hhhh", "vvv",
-        [((2, 2, C, N), BF16), ((2, C, 9 * C), BF16), ((2, C, N), F32), ((2, C, N), F32)],
-        4, 6 * 10**8, 2 * 10**6,
+    give, ms, u, g, lc = call(
+        give_kernel,
+        (shape((C, 2 * N + WIDE), BF16), shape((2, 3 * C, 3 * C), BF16), shape((2, C, N), BF16), image, image),
+        "hhhh", "vvvvv", [((2, C, 9 * C), BF16), ((2, C, N), BF16), ((C, N), F32), ((C, N), F32)],
+        9, 3 * 10**8, 2 * 10**6,
     )(*[pltpu.with_memory_space_constraint(x, pltpu.HBM) for x in (states, weights, guess, loss)])
     got = lax.ppermute(give, "section", swap)
+    keep = call(keep_kernel, shape((C, 2 * N), BF16), "vvvv", "v", [], 0, 3 * 10**8, 10**6)(ms, u, g, lc)
     pairs, odd = call(
         merge_kernel, (shape((chips, C, LEAD + N), BF16), image16), "vvv", "vv", [], 0, 10**8, 3 * 10**6,
     )(keep, got, ms)
@@ -291,7 +309,7 @@
 
     sums = call(own_kernel, shape((2, 3 * C, 3 * C), F32), "vvvv", "v", [], 0, 4 * 10**8, 10**6)(ms, acts, slopes, mine)
     grads = call(
-        other_kernel, shape((nb, 2 * (C // nb), 9 * C), BF16), "vvvvv", "v", [], 0, 4 * 10**8, 10**6
+        other_kernel, shape((nb, 9 * (C // nb), 2 * C), BF16), "vvvvv", "v", [], 0, 4 * 10**8, 10**6
     )(ms, acts, slopes, theirs, sums)
     starts = call(start_kernel, shape((1, 2, C, N), F32), "vvvv", "v", [], 0, 6 * 10**8, 3 * 10**6)(
         ms, slopes, mine, theirs

time: 75.8 us -> 75.1 us (level)
  waiting for transfers between devices: 15.6 us -> 14.7 us
    ppermute x1, waiting for transfers between devices: 1.64 us -> 0.78 us  [shards(): got = lax.ppermute(give, 'section', swap)]
    pallas_call x2 -> x3, Pallas kernels: 4.53 us -> 4.63 us  [the longest x1 2.17 us: shards(): call(give_kernel, (shape((C, 2 * N + WIDE), BF16), shape((2, 3 * C, 3 * C...]
  transfers between devices with their start and end apart: 4 -> 4, of which waited for: 4 -> 4; matrix products, arithmetic and copies ran while one was open for 0% -> 0% of each run, Pallas kernels for 5% -> 6%
where the time goes in v1:
time: 75.1 us; the launch traced here: 74.9 us
  blocking collectives  31.6 us (42%)
  Pallas kernels  15.3 us (20%)
  waiting for transfers between devices  14.7 us (20%)
  starting transfers between devices  12.5 us (17%)
    all_to_all x1, blocking collectives, shards(): lax.all_to_all(pairs, 'section', 0, 0, axis_index_groups=groups, tiled=True)  31.6 us
    all_to_all x1, starting transfers between devices, shards(): grads = lax.all_to_all(grads, 'batch', 0, 0, tiled=True)  11 us
    all_to_all x1, waiting for transfers between devices, shards(): grads = lax.all_to_all(grads, 'batch', 0, 0, tiled=True)  8.23 us
    ppermute x1, waiting for transfers between devices, shards(): lax.ppermute(last, 'section', [(i, i - half) for i in range(half, section...  5.13 us
    pallas_call x1, Pallas kernels, shards(): call(lower_kernel, (image, image), 'vvvv', 'vv', [((C, N), F32), ((C, N),...  3.23 us
    pallas_call x1, Pallas kernels, shards(): call(upper_kernel, image16, 'v', 'v', [], 0, 10 ** 9, 2 * 10 ** 6)(packed)  2.62 us
    pallas_call x1, Pallas kernels, shards(): call(give_kernel, (shape((C, 2 * N + WIDE), BF16), shape((2, 3 * C, 3 * C...  2.17 us
    pallas_call x1, Pallas kernels, shards(): call(start_kernel, shape((1, 2, C, N), F32), 'vvvv', 'v', [], 0, 6 * 10 *...  2.14 us
  transfers between devices with their start and end apart: 4, of which 4 were waited for; matrix products, arithmetic and copies ran while one was open for 0% of the time, Pallas kernels for 6%

profile of v1, /device:TPU:32, one launch (start us, length us, event | category | flops | bytes accessed | tf_op | source)
XLA Modules:
  0.0 74.9 jit_solution(4091037931776713387)
XLA Ops:
  0.6 2.2 %shard_map.59 = (bf16[64,2688]{1,0:T(8,128)(2,1)S(1)}, bf16[2,192,192]{2,1,0:T(8,128)(2,1)S(1)}, bf16[2,64,1024]{2,1,0:T(8,128)(2,1)S(1)}, f32[64,1024]{1,0:T(8,128)S(1)}, f32[64,1024]{1,0:T(8,128)S(1)}) custom-call(bf16[2,2,64,1024]{3,2,1,0:T(8,128)(2,1)} %states.3, bf16[2,64,576]{2,1,0:T(8,128)(2,1)} %weights.1, f32[1,2,64,1024]{3,2,1,0:T(8,128)} %guess.1, ...), custom_call_target="tpu_custom_call" | custom-call | flops 300000000 | bytes 2000000 | tf_op jit(solution)/shard_map/pallas_call | solution.py:284
  2.8 0.1 collective-permute-start
  2.9 0.8 %shard_map.61.keep = bf16[64,2048]{1,0:T(8,128)(2,1)S(1)} custom-call(bf16[2,192,192]{2,1,0:T(8,128)(2,1)S(1)} %get-tuple-element.14.ms, bf16[2,64,1024]{2,1,0:T(8,128)(2,1)S(1)} %get-tuple-element.16.u, f32[64,1024]{1,0:T(8,128)S(1)} %get-tuple-element.17.g, f32[64,1024]{1,0:T(8,128)S(1)} %get-tuple-element.18.lc), custom_call_target="tpu_custom_call" | custom-call | flops 300000000 | bytes 1000000 | tf_op jit(solution)/shard_map/pallas_call | solution.py:291
  3.8 0.8 %collective-permute-done.got = bf16[64,2688]{1,0:T(8,128)(2,1)S(1)} collective-permute-done((bf16[64,2688]{1,0:T(8,128)(2,1)S(1)}, bf16[64,2688]{1,0:T(8,128)(2,1)S(1)}, u32[]{:S(2)}, u32[]{:S(2)}) %collective-permute-start) | collective-permute-done | bytes 344096 | tf_op jit(solution)/shard_map/ppermute | solution.py:290
  4.5 0.5 shard_map.62
  5.1 31.6 %all_to_all.10.packed = bf16[4,64,4224]{2,1,0:T(8,128)(2,1)S(1)} all-to-all(bf16[4,64,4224]{2,1,0:T(8,128)(2,1)S(1)} %get-tuple-element.20), channel_id=1, replica_groups={{0,32,64,96},{16,48,80,112},{128,160,192,224},{144,176,208,240},{1,33,6..., dimensions={0} | all-to-all | bytes 4325376 | tf_op jit(solution)/shard_map/all_to_all | solution.py:296
  36.7 0.0 copy-start
  36.7 0.0 copy-start.1
  36.7 2.6 %shard_map.63 = bf16[64,1024]{1,0:T(8,128)(2,1)S(1)} custom-call(bf16[4,64,4224]{2,1,0:T(8,128)(2,1)S(1)} %all_to_all.10.packed), custom_call_target="tpu_custom_call" | custom-call | flops 1000000000 | bytes 2000000 | tf_op jit(solution)/shard_map/pallas_call | solution.py:302
  39.3 1.3 %collective-permute-start.1 = (bf16[64,1024]{1,0:T(8,128)(2,1)S(1)}, bf16[64,1024]{1,0:T(8,128)(2,1)S(1)}, u32[]{:S(2)}, u32[]{:S(2)}) collective-permute-start(bf16[64,1024]{1,0:T(8,128)(2,1)S(1)} %shard_map.63), channel_id=1, source_target_pairs={{128,0},{144,16},{160,32},{176,48},{192,64},{208,80},{224,96},{240... | collective-permute-start | bytes 393224 | tf_op jit(solution)/shard_map/ppermute | solution.py:303
  40.6 0.0 copy-done
  40.6 0.0 copy-done.1
  40.6 0.4 shard_map.60
  41.0 5.1 %collective-permute-done.1.start = bf16[64,1024]{1,0:T(8,128)(2,1)S(1)} collective-permute-done((bf16[64,1024]{1,0:T(8,128)(2,1)S(1)}, bf16[64,1024]{1,0:T(8,128)(2,1)S(1)}, u32[]{:S(2)}, u32[]{:S(2)}) %collective-permute-start.1) | collective-permute-done | bytes 131104 | tf_op jit(solution)/shard_map/ppermute | solution.py:303
  46.2 3.2 %shard_map.64 = (f32[64,1024]{1,0:T(8,128)S(1)}, f32[64,1024]{1,0:T(8,128)S(1)}) custom-call(bf16[64,1024]{1,0:T(8,128)(2,1)S(1)} %collective-permute-done.1.start, bf16[4,64,4224]{2,1,0:T(8,128)(2,1)S(1)} %all_to_all.10.packed, bf16[64,1024]{1,0:T(8,128)(2,1)S(1)} %get-tuple-element.21.odd, f32[64,1024]{1,0:T(8,128)S(1)} %get-tuple-element.22.base), custom_call_target="tpu_custom_call" | custom-call | flops 1200000000 | bytes 2000000 | tf_op jit(solution)/shard_map/pallas_call | solution.py:304
  49.4 0.1 collective-permute-start.2
  49.5 0.9 %shard_map.66.sums = f32[2,192,192]{2,1,0:T(8,128)S(1)} custom-call(bf16[2,192,192]{2,1,0:T(8,128)(2,1)S(1)} %get-tuple-element.14.ms, bf16[2,2,192,1024]{3,2,1,0:T(8,128)(2,1)S(1)} %get-tuple-element.25.acts, f32[2,2,64,1024]{3,2,1,0:T(8,128)S(1)} %get-tuple-element.15.slopes, f32[64,1024]{1,0:T(8,128)S(1)} %get-tuple-element.23.mine), custom_call_target="tpu_custom_call" | custom-call | flops 400000000 | bytes 1000000 | tf_op jit(solution)/shard_map/pallas_call | solution.py:310
  50.5 0.6 collective-permute-done.2.theirs.other
  51.0 1.6 %shard_map.67 = bf16[16,36,128]{2,1,0:T(8,128)(2,1)} custom-call(bf16[2,192,192]{2,1,0:T(8,128)(2,1)S(1)} %get-tuple-element.14.ms, bf16[2,2,192,1024]{3,2,1,0:T(8,128)(2,1)S(1)} %get-tuple-element.25.acts, f32[2,2,64,1024]{3,2,1,0:T(8,128)S(1)} %get-tuple-element.15.slopes, f32[64,1024]{1,0:T(8,128)S(1)} %collective-permute-done.2.theirs.other, ...), custom_call_target="tpu_custom_call" | custom-call | flops 400000000 | bytes 1000000 | tf_op jit(solution)/shard_map/pallas_call | solution.py:311
  52.7 11.0 %all-to-all-start.1 = ((bf16[16,36,128]{2,1,0:T(8,128)(2,1)}), bf16[16,36,128]{2,1,0:T(8,128)(2,1)S(1)}, u32[]{:S(2)}, u32[]{:S(2)}) async-start(bf16[16,36,128]{2,1,0:T(8,128)(2,1)} %shard_map.67), calls=%async_computation.1 | async-start | bytes 327680 | tf_op jit(solution)/shard_map/all_to_all | solution.py:317
  63.7 2.1 %shard_map.65 = f32[1,2,64,1024]{3,2,1,0:T(8,128)} custom-call(bf16[2,192,192]{2,1,0:T(8,128)(2,1)S(1)} %get-tuple-element.14.ms, f32[2,2,64,1024]{3,2,1,0:T(8,128)S(1)} %get-tuple-element.15.slopes, f32[64,1024]{1,0:T(8,128)S(1)} %get-tuple-element.23.mine, f32[64,1024]{1,0:T(8,128)S(1)} %collective-permute-done.2.theirs.other), custom_call_target="tpu_custom_call" | custom-call | flops 600000000 | bytes 3000000 | tf_op jit(solution)/shard_map/pallas_call | solution.py:314
  65.8 8.2 %all-to-all-done.1.parts = bf16[16,36,128]{2,1,0:T(8,128)(2,1)S(1)} async-done(((bf16[16,36,128]{2,1,0:T(8,128)(2,1)}), bf16[16,36,128]{2,1,0:T(8,128)(2,1)S(1)}, u32[]{:S(2)}, u32[]{:S(2)}) %all-to-all-start.1) | async-done | bytes 147488 | tf_op jit(solution)/shard_map/all_to_all | solution.py:317
  74.1 0.8 %shard_map.68 = f32[2,2304]{1,0:T(2,128)} custom-call(bf16[16,36,128]{2,1,0:T(8,128)(2,1)S(1)} %all-to-all-done.1.parts), custom_call_target="tpu_custom_call" | custom-call | flops 1000000 | bytes 1000000 | tf_op jit(solution)/shard_map/pallas_call | solution.py:318
Async XLA Ops:
  2.8 1.7 %collective-permute-start = (bf16[64,2688]{1,0:T(8,128)(2,1)S(1)}, bf16[64,2688]{1,0:T(8,128)(2,1)S(1)}, u32[]{:S(2)}, u32[]{:S(2)}) collective-permute-start(bf16[64,2688]{1,0:T(8,128)(2,1)S(1)} %get-tuple-element.19), channel_id=1, source_target_pairs={{0,16},{16,0},{32,48},{48,32},{64,80},{80,64},{96,112},{112,96},{1... | collective-permute-start | bytes 1032200 | tf_op jit(solution)/shard_map/ppermute | solution.py:290
  36.7 3.9 %copy-start = (bf16[2,2,64,1024]{3,2,1,0:T(8,128)(2,1)S(1)}, bf16[2,2,64,1024]{3,2,1,0:T(8,128)(2,1)}, u32[]{:S(2)}) copy-start(bf16[2,2,64,1024]{3,2,1,0:T(8,128)(2,1)} %states.3) | copy-start | bytes 1572868
  36.7 3.9 %copy-start.1 = (f32[2,64,1024]{2,1,0:T(8,128)S(1)}, f32[2,64,1024]{2,1,0:T(8,128)}, u32[]{:S(2)}) copy-start(f32[2,64,1024]{2,1,0:T(8,128)} %loss.3) | copy-start | bytes 1572868
  39.3 6.9 %collective-permute-start.1 = (bf16[64,1024]{1,0:T(8,128)(2,1)S(1)}, bf16[64,1024]{1,0:T(8,128)(2,1)S(1)}, u32[]{:S(2)}, u32[]{:S(2)}) collective-permute-start(bf16[64,1024]{1,0:T(8,128)(2,1)S(1)} %shard_map.63), channel_id=1, source_target_pairs={{128,0},{144,16},{160,32},{176,48},{192,64},{208,80},{224,96},{240... | collective-permute-start | bytes 393224 | tf_op jit(solution)/shard_map/ppermute | solution.py:303
  49.4 1.6 %collective-permute-start.2 = (f32[64,1024]{1,0:T(8,128)S(1)}, f32[64,1024]{1,0:T(8,128)S(1)}, u32[]{:S(2)}, u32[]{:S(2)}) collective-permute-start(f32[64,1024]{1,0:T(8,128)S(1)} %get-tuple-element.24), channel_id=1, source_target_pairs={{0,16},{16,0},{32,48},{48,32},{64,80},{80,64},{96,112},{112,96},{1... | collective-permute-start | bytes 786440 | tf_op jit(solution)/shard_map/ppermute | solution.py:308
  52.7 21.4 %all-to-all-start.1 = ((bf16[16,36,128]{2,1,0:T(8,128)(2,1)}), bf16[16,36,128]{2,1,0:T(8,128)(2,1)S(1)}, u32[]{:S(2)}, u32[]{:S(2)}) async-start(bf16[16,36,128]{2,1,0:T(8,128)(2,1)} %shard_map.67), calls=%async_computation.1 | async-start | bytes 327680 | tf_op jit(solution)/shard_map/all_to_all | solution.py:317

commit v2 on v1

--- a/solution.py
+++ b/solution.py
@@ -207,19 +207,24 @@
     other[...] = jnp.where(even, at_high, at_low)
 
 
-def finish(i, ms, acts, slopes, v):
+def finish(i, ms, acts, slopes, v, start, starts, sems):
     x3 = cols3(v)
     first = lax.dot_general(x3, acts[1, i], (((1,), (1,)), ((), ())), preferred_element_type=F32)
-    x3 = cols3(v + slopes[1, i] * conv(ms[1], x3))
-    return lax.dot_general(x3, acts[0, i], (((1,), (1,)), ((), ())), preferred_element_type=F32), first
-
-
-def own_kernel(ms, acts, slopes, mine, sums):
-    sums[0], sums[1] = finish(core(), ms, acts, slopes, mine[...])
-
-
-def other_kernel(ms, acts, slopes, other, sums, grads):
-    products = finish(1 - core(), ms, acts, slopes, other[...])
+    v = v + slopes[1, i] * conv(ms[1], x3)
+    x3 = cols3(v)
+    start[...] = v + slopes[0, i] * conv(ms[0], x3)
+    sent = moves([(start, starts.at[0, i])], sems)
+    return lax.dot_general(x3, acts[0, i], (((1,), (1,)), ((), ())), preferred_element_type=F32), first, sent
+
+
+def own_kernel(ms, acts, slopes, mine, sums, starts, start, sems):
+    sums[0], sums[1], sent = finish(core(), ms, acts, slopes, mine[...], start, starts, sems)
+    settle(sent)
+
+
+def other_kernel(ms, acts, slopes, other, sums, begun, grads, starts, start, sems):
+    del begun
+    *products, sent = finish(1 - core(), ms, acts, slopes, other[...], start, starts, sems)
     parts = grads.shape[0]
     rows = C // parts
     g = [(sums[layer] + products[layer]) * H for layer in range(2)]
@@ -231,14 +236,7 @@
             for piece in (g[0][:, :cut], g[1][:, :cut], rest) for b in range(3)
         ]
         grads[d] = jnp.concatenate(pieces, axis=0).astype(grads.dtype)
-
-
-def start_kernel(ms, slopes, mine, theirs, starts):
-    for i, lam in ((core(), mine), (1 - core(), theirs)):
-        v = lam[...]
-        for layer in (1, 0):
-            v = v + slopes[layer, i] * conv(ms[layer], cols3(v))
-        starts[0, i] = v
+    settle(sent)
 
 
 def total_kernel(parts, out):
@@ -256,7 +254,7 @@
         out[layer : layer + 1, :] = jnp.concatenate([wide[r : r + 1] for r in range(rows)], axis=1)
 
 
-def call(kernel, outs, where_in, where_out, scratch, n_sems, flops, moved, grant=16 << 20):
+def call(kernel, outs, where_in, where_out, scratch, n_sems, flops, moved, grant=16 << 20, aliases={}):
     spaces = {"s": pltpu.SMEM, "v": pltpu.VMEM, "h": pltpu.HBM}
     specs = lambda text: [pl.BlockSpec(memory_space=spaces[k]) for k in text]
     out_specs = specs(where_out)
@@ -267,6 +265,7 @@
         out_specs=tuple(out_specs) if isinstance(outs, tuple) else out_specs[0],
         scratch_shapes=[pltpu.VMEM(*one) for one in scratch]
         + ([pltpu.SemaphoreType.DMA((n_sems,))] if n_sems else []),
+        input_output_aliases=aliases,
         cost_estimate=pl.CostEstimate(flops=flops, bytes_accessed=moved, transcendentals=0),
         compiler_params=pltpu.CompilerParams(vmem_limit_bytes=grant),
     )
@@ -307,13 +306,14 @@
     )(carried, packed, odd, base)
     theirs = lax.ppermute(other, "section", swap)
 
-    sums = call(own_kernel, shape((2, 3 * C, 3 * C), F32), "vvvv", "v", [], 0, 4 * 10**8, 10**6)(ms, acts, slopes, mine)
-    grads = call(
-        other_kernel, shape((nb, 9 * (C // nb), 2 * C), BF16), "vvvvv", "v", [], 0, 4 * 10**8, 10**6
-    )(ms, acts, slopes, theirs, sums)
-    starts = call(start_kernel, shape((1, 2, C, N), F32), "vvvv", "v", [], 0, 6 * 10**8, 3 * 10**6)(
-        ms, slopes, mine, theirs
-    )
+    whole = shape((1, 2, C, N), F32)
+    sums, starts = call(
+        own_kernel, (shape((2, 3 * C, 3 * C), F32), whole), "vvvv", "vh", [((C, N), F32)], 1, 4 * 10**8, 10**6
+    )(ms, acts, slopes, mine)
+    grads, starts = call(
+        other_kernel, (shape((nb, 9 * (C // nb), 2 * C), BF16), whole), "vvvvvh", "vh", [((C, N), F32)], 1,
+        4 * 10**8, 10**6, aliases={5: 1},
+    )(ms, acts, slopes, theirs, sums, starts)
     grads = lax.all_to_all(grads, "batch", 0, 0, tiled=True)
     total = call(total_kernel, shape((2, 9 * C * C // nb), F32), "v", "v", [], 0, 10**6, 10**6)(grads)
     return starts, total

time: 75.1 us -> 75.5 us (level)
  blocking collectives: 31.6 us -> 53 us
  starting transfers between devices: 12.5 us -> 1.48 us
  waiting for transfers between devices: 14.7 us -> 5.92 us
  Pallas kernels: 15.3 us -> 14.1 us
    all_to_all x0 -> x1, blocking collectives: none -> 21.4 us  [shards(): grads = lax.all_to_all(grads, 'batch', 0, 0, tiled=True)]
    all_to_all x1 -> x0, starting transfers between devices: 11 us -> none  [shards(): grads = lax.all_to_all(grads, 'batch', 0, 0, tiled=True)]
    all_to_all x1 -> x0, waiting for transfers between devices: 8.23 us -> none  [shards(): grads = lax.all_to_all(grads, 'batch', 0, 0, tiled=True)]
    pallas_call x3 -> x2, Pallas kernels: 4.7 us -> 3.49 us  [the longest x1 1.75 us: shards(): call(other_kernel, (shape((nb, 9 * (C // nb), 2 * C), BF16), whole), 'vvv...]
  transfers between devices with their start and end apart: 4 -> 3, of which waited for: 4 -> 2; matrix products, arithmetic and copies ran while one was open for 0% -> 0% of each run, Pallas kernels for 6% -> 4%
where the time goes in v2:
time: 75.5 us; the launch traced here: 75.3 us
  blocking collectives  53 us (70%)
  Pallas kernels  14.1 us (19%)
  waiting for transfers between devices  5.92 us (8%)
  starting transfers between devices  1.48 us (2%)
    all_to_all x1, blocking collectives, shards(): lax.all_to_all(pairs, 'section', 0, 0, axis_index_groups=groups, tiled=True)  31.6 us
    all_to_all x1, blocking collectives, shards(): grads = lax.all_to_all(grads, 'batch', 0, 0, tiled=True)  21.4 us
    ppermute x1, waiting for transfers between devices, shards(): lax.ppermute(last, 'section', [(i, i - half) for i in range(half, section...  5.13 us
    pallas_call x1, Pallas kernels, shards(): call(lower_kernel, (image, image), 'vvvv', 'vv', [((C, N), F32), ((C, N),...  3.23 us
    pallas_call x1, Pallas kernels, shards(): call(upper_kernel, image16, 'v', 'v', [], 0, 10 ** 9, 2 * 10 ** 6)(packed)  2.62 us
    pallas_call x1, Pallas kernels, shards(): call(give_kernel, (shape((C, 2 * N + WIDE), BF16), shape((2, 3 * C, 3 * C...  2.17 us
    pallas_call x1, Pallas kernels, shards(): call(other_kernel, (shape((nb, 9 * (C // nb), 2 * C), BF16), whole), 'vvv...  1.75 us
    pallas_call x1, Pallas kernels, shards(): call(own_kernel, (shape((2, 3 * C, 3 * C), F32), whole), 'vvvv', 'vh', [(...  1.74 us
  transfers between devices with their start and end apart: 3, of which 2 were waited for; matrix products, arithmetic and copies ran while one was open for 0% of the time, Pallas kernels for 4%

profile of v2, /device:TPU:32, one launch (start us, length us, event | category | flops | bytes accessed | tf_op | source)
XLA Modules:
  0.0 75.3 jit_solution(8353575861883263113)
XLA Ops:
  0.6 2.2 %shard_map.59 = (bf16[64,2688]{1,0:T(8,128)(2,1)S(1)}, bf16[2,192,192]{2,1,0:T(8,128)(2,1)S(1)}, bf16[2,64,1024]{2,1,0:T(8,128)(2,1)S(1)}, f32[64,1024]{1,0:T(8,128)S(1)}, f32[64,1024]{1,0:T(8,128)S(1)}) custom-call(bf16[2,2,64,1024]{3,2,1,0:T(8,128)(2,1)} %states.3, bf16[2,64,576]{2,1,0:T(8,128)(2,1)} %weights.1, f32[1,2,64,1024]{3,2,1,0:T(8,128)} %guess.1, ...), custom_call_target="tpu_custom_call" | custom-call | flops 300000000 | bytes 2000000 | tf_op jit(solution)/shard_map/pallas_call | solution.py:283
  2.8 0.1 collective-permute-start
  2.9 0.8 %shard_map.61.keep = bf16[64,2048]{1,0:T(8,128)(2,1)S(1)} custom-call(bf16[2,192,192]{2,1,0:T(8,128)(2,1)S(1)} %get-tuple-element.18.ms, bf16[2,64,1024]{2,1,0:T(8,128)(2,1)S(1)} %get-tuple-element.21.u, f32[64,1024]{1,0:T(8,128)S(1)} %get-tuple-element.22.g, f32[64,1024]{1,0:T(8,128)S(1)} %get-tuple-element.23.lc), custom_call_target="tpu_custom_call" | custom-call | flops 300000000 | bytes 1000000 | tf_op jit(solution)/shard_map/pallas_call | solution.py:290
  3.8 0.8 %collective-permute-done.got = bf16[64,2688]{1,0:T(8,128)(2,1)S(1)} collective-permute-done((bf16[64,2688]{1,0:T(8,128)(2,1)S(1)}, bf16[64,2688]{1,0:T(8,128)(2,1)S(1)}, u32[]{:S(2)}, u32[]{:S(2)}) %collective-permute-start) | collective-permute-done | bytes 344096 | tf_op jit(solution)/shard_map/ppermute | solution.py:289
  4.5 0.5 shard_map.62
  5.1 31.6 %all_to_all.10.packed = bf16[4,64,4224]{2,1,0:T(8,128)(2,1)S(1)} all-to-all(bf16[4,64,4224]{2,1,0:T(8,128)(2,1)S(1)} %get-tuple-element.25), channel_id=1, replica_groups={{0,32,64,96},{16,48,80,112},{128,160,192,224},{144,176,208,240},{1,33,6..., dimensions={0} | all-to-all | bytes 4325376 | tf_op jit(solution)/shard_map/all_to_all | solution.py:295
  36.7 0.0 copy-start
  36.7 0.0 copy-start.1
  36.7 2.6 %shard_map.63 = bf16[64,1024]{1,0:T(8,128)(2,1)S(1)} custom-call(bf16[4,64,4224]{2,1,0:T(8,128)(2,1)S(1)} %all_to_all.10.packed), custom_call_target="tpu_custom_call" | custom-call | flops 1000000000 | bytes 2000000 | tf_op jit(solution)/shard_map/pallas_call | solution.py:301
  39.3 1.3 %collective-permute-start.1 = (bf16[64,1024]{1,0:T(8,128)(2,1)S(1)}, bf16[64,1024]{1,0:T(8,128)(2,1)S(1)}, u32[]{:S(2)}, u32[]{:S(2)}) collective-permute-start(bf16[64,1024]{1,0:T(8,128)(2,1)S(1)} %shard_map.63), channel_id=1, source_target_pairs={{128,0},{144,16},{160,32},{176,48},{192,64},{208,80},{224,96},{240... | collective-permute-start | bytes 393224 | tf_op jit(solution)/shard_map/ppermute | solution.py:302
  40.6 0.0 copy-done
  40.6 0.0 copy-done.1
  40.6 0.4 shard_map.60
  41.0 5.1 %collective-permute-done.1.start = bf16[64,1024]{1,0:T(8,128)(2,1)S(1)} collective-permute-done((bf16[64,1024]{1,0:T(8,128)(2,1)S(1)}, bf16[64,1024]{1,0:T(8,128)(2,1)S(1)}, u32[]{:S(2)}, u32[]{:S(2)}) %collective-permute-start.1) | collective-permute-done | bytes 131104 | tf_op jit(solution)/shard_map/ppermute | solution.py:302
  46.2 3.2 %shard_map.64 = (f32[64,1024]{1,0:T(8,128)S(1)}, f32[64,1024]{1,0:T(8,128)S(1)}) custom-call(bf16[64,1024]{1,0:T(8,128)(2,1)S(1)} %collective-permute-done.1.start, bf16[4,64,4224]{2,1,0:T(8,128)(2,1)S(1)} %all_to_all.10.packed, bf16[64,1024]{1,0:T(8,128)(2,1)S(1)} %get-tuple-element.26.odd, f32[64,1024]{1,0:T(8,128)S(1)} %get-tuple-element.27.base), custom_call_target="tpu_custom_call" | custom-call | flops 1200000000 | bytes 2000000 | tf_op jit(solution)/shard_map/pallas_call | solution.py:303
  49.4 0.1 collective-permute-start.2
  49.5 1.7 %shard_map.65 = (f32[2,192,192]{2,1,0:T(8,128)S(1)}, f32[1,2,64,1024]{3,2,1,0:T(8,128)}) custom-call(bf16[2,192,192]{2,1,0:T(8,128)(2,1)S(1)} %get-tuple-element.18.ms, bf16[2,2,192,1024]{3,2,1,0:T(8,128)(2,1)S(1)} %get-tuple-element.19.acts, f32[2,2,64,1024]{3,2,1,0:T(8,128)S(1)} %get-tuple-element.20.slopes, f32[64,1024]{1,0:T(8,128)S(1)} %get-tuple-element.29.mine), custom_call_target="tpu_custom_call" | custom-call | flops 400000000 | bytes 1000000 | tf_op jit(solution)/shard_map/pallas_call | solution.py:310
  51.3 0.0 collective-permute-done.2.other
  51.3 1.8 %shard_map.66 = (bf16[16,36,128]{2,1,0:T(8,128)(2,1)S(1)}, f32[1,2,64,1024]{3,2,1,0:T(8,128)}) custom-call(bf16[2,192,192]{2,1,0:T(8,128)(2,1)S(1)} %get-tuple-element.18.ms, bf16[2,2,192,1024]{3,2,1,0:T(8,128)(2,1)S(1)} %get-tuple-element.19.acts, f32[2,2,64,1024]{3,2,1,0:T(8,128)S(1)} %get-tuple-element.20.slopes, ...), custom_call_target="tpu_custom_call", output_to_operand_aliasing={{1}: (5, {})} | custom-call | flops 400000000 | bytes 1000000 | tf_op jit(solution)/shard_map/pallas_call | solution.py:313
  53.0 21.4 %all_to_all.11.parts = bf16[16,36,128]{2,1,0:T(8,128)(2,1)S(1)} all-to-all(bf16[16,36,128]{2,1,0:T(8,128)(2,1)S(1)} %get-tuple-element.33), channel_id=1, replica_groups=mesh['section'=16,'batch'=16] {'batch'}, dimensions={0} | all-to-all | bytes 294912 | tf_op jit(solution)/shard_map/all_to_all | solution.py:317
  74.5 0.8 %shard_map.67 = f32[2,2304]{1,0:T(2,128)} custom-call(bf16[16,36,128]{2,1,0:T(8,128)(2,1)S(1)} %all_to_all.11.parts), custom_call_target="tpu_custom_call" | custom-call | flops 1000000 | bytes 1000000 | tf_op jit(solution)/shard_map/pallas_call | solution.py:318
Async XLA Ops:
  2.8 1.7 %collective-permute-start = (bf16[64,2688]{1,0:T(8,128)(2,1)S(1)}, bf16[64,2688]{1,0:T(8,128)(2,1)S(1)}, u32[]{:S(2)}, u32[]{:S(2)}) collective-permute-start(bf16[64,2688]{1,0:T(8,128)(2,1)S(1)} %get-tuple-element.24), channel_id=1, source_target_pairs={{0,16},{16,0},{32,48},{48,32},{64,80},{80,64},{96,112},{112,96},{1... | collective-permute-start | bytes 1032200 | tf_op jit(solution)/shard_map/ppermute | solution.py:289
  36.7 3.9 %copy-start = (bf16[2,2,64,1024]{3,2,1,0:T(8,128)(2,1)S(1)}, bf16[2,2,64,1024]{3,2,1,0:T(8,128)(2,1)}, u32[]{:S(2)}) copy-start(bf16[2,2,64,1024]{3,2,1,0:T(8,128)(2,1)} %states.3) | copy-start | bytes 1572868
  36.7 3.9 %copy-start.1 = (f32[2,64,1024]{2,1,0:T(8,128)S(1)}, f32[2,64,1024]{2,1,0:T(8,128)}, u32[]{:S(2)}) copy-start(f32[2,64,1024]{2,1,0:T(8,128)} %loss.3) | copy-start | bytes 1572868
  39.3 6.9 %collective-permute-start.1 = (bf16[64,1024]{1,0:T(8,128)(2,1)S(1)}, bf16[64,1024]{1,0:T(8,128)(2,1)S(1)}, u32[]{:S(2)}, u32[]{:S(2)}) collective-permute-start(bf16[64,1024]{1,0:T(8,128)(2,1)S(1)} %shard_map.63), channel_id=1, source_target_pairs={{128,0},{144,16},{160,32},{176,48},{192,64},{208,80},{224,96},{240... | collective-permute-start | bytes 393224 | tf_op jit(solution)/shard_map/ppermute | solution.py:302
  49.4 1.8 %collective-permute-start.2 = (f32[64,1024]{1,0:T(8,128)S(1)}, f32[64,1024]{1,0:T(8,128)S(1)}, u32[]{:S(2)}, u32[]{:S(2)}) collective-permute-start(f32[64,1024]{1,0:T(8,128)S(1)} %get-tuple-element.28), channel_id=1, source_target_pairs={{0,16},{16,0},{32,48},{48,32},{64,80},{80,64},{96,112},{112,96},{1... | collective-permute-start | bytes 786440 | tf_op jit(solution)/shard_map/ppermute | solution.py:307

commit v3 on v2

--- a/solution.py
+++ b/solution.py
@@ -59,7 +59,8 @@
 
 
 def conv(m, x3):
-    y = jnp.dot(m, x3, preferred_element_type=F32)
+    halves = [x3[:, : N // 2], x3[:, N // 2 :]]
+    y = jnp.concatenate([jnp.dot(m, half, preferred_element_type=F32) for half in halves], axis=1)
     low = row_down(y[:C].astype(BF16))
     high = row_up(y[2 * C :].astype(BF16))
     return y[C : 2 * C] + low.astype(F32) + high.astype(F32)
@@ -207,24 +208,23 @@
     other[...] = jnp.where(even, at_high, at_low)
 
 
-def finish(i, ms, acts, slopes, v, start, starts, sems):
+def finish(i, ms, acts, slopes, v, start):
     x3 = cols3(v)
     first = lax.dot_general(x3, acts[1, i], (((1,), (1,)), ((), ())), preferred_element_type=F32)
     v = v + slopes[1, i] * conv(ms[1], x3)
     x3 = cols3(v)
     start[...] = v + slopes[0, i] * conv(ms[0], x3)
-    sent = moves([(start, starts.at[0, i])], sems)
-    return lax.dot_general(x3, acts[0, i], (((1,), (1,)), ((), ())), preferred_element_type=F32), first, sent
-
-
-def own_kernel(ms, acts, slopes, mine, sums, starts, start, sems):
-    sums[0], sums[1], sent = finish(core(), ms, acts, slopes, mine[...], start, starts, sems)
-    settle(sent)
+    return lax.dot_general(x3, acts[0, i], (((1,), (1,)), ((), ())), preferred_element_type=F32), first
+
+
+def own_kernel(ms, acts, slopes, mine, sums, start):
+    sums[0], sums[1] = finish(core(), ms, acts, slopes, mine[...], start)
 
 
 def other_kernel(ms, acts, slopes, other, sums, begun, grads, starts, start, sems):
-    del begun
-    *products, sent = finish(1 - core(), ms, acts, slopes, other[...], start, starts, sems)
+    sent = moves([(begun, starts.at[0, core()])], sems)
+    products = finish(1 - core(), ms, acts, slopes, other[...], start)
+    sent += moves([(start, starts.at[0, 1 - core()])], sems, 1)
     parts = grads.shape[0]
     rows = C // parts
     g = [(sums[layer] + products[layer]) * H for layer in range(2)]
@@ -254,7 +254,7 @@
         out[layer : layer + 1, :] = jnp.concatenate([wide[r : r + 1] for r in range(rows)], axis=1)
 
 
-def call(kernel, outs, where_in, where_out, scratch, n_sems, flops, moved, grant=16 << 20, aliases={}):
+def call(kernel, outs, where_in, where_out, scratch, n_sems, flops, moved, grant=16 << 20):
     spaces = {"s": pltpu.SMEM, "v": pltpu.VMEM, "h": pltpu.HBM}
     specs = lambda text: [pl.BlockSpec(memory_space=spaces[k]) for k in text]
     out_specs = specs(where_out)
@@ -265,7 +265,6 @@
         out_specs=tuple(out_specs) if isinstance(outs, tuple) else out_specs[0],
         scratch_shapes=[pltpu.VMEM(*one) for one in scratch]
         + ([pltpu.SemaphoreType.DMA((n_sems,))] if n_sems else []),
-        input_output_aliases=aliases,
         cost_estimate=pl.CostEstimate(flops=flops, bytes_accessed=moved, transcendentals=0),
         compiler_params=pltpu.CompilerParams(vmem_limit_bytes=grant),
     )
@@ -306,14 +305,13 @@
     )(carried, packed, odd, base)
     theirs = lax.ppermute(other, "section", swap)
 
-    whole = shape((1, 2, C, N), F32)
-    sums, starts = call(
-        own_kernel, (shape((2, 3 * C, 3 * C), F32), whole), "vvvv", "vh", [((C, N), F32)], 1, 4 * 10**8, 10**6
+    sums, begun = call(
+        own_kernel, (shape((2, 3 * C, 3 * C), F32), image), "vvvv", "vv", [], 0, 4 * 10**8, 10**6
     )(ms, acts, slopes, mine)
     grads, starts = call(
-        other_kernel, (shape((nb, 9 * (C // nb), 2 * C), BF16), whole), "vvvvvh", "vh", [((C, N), F32)], 1,
-        4 * 10**8, 10**6, aliases={5: 1},
-    )(ms, acts, slopes, theirs, sums, starts)
+        other_kernel, (shape((nb, 9 * (C // nb), 2 * C), BF16), shape((1, 2, C, N), F32)), "vvvvvv", "vh",
+        [((C, N), F32)], 2, 4 * 10**8, 10**6,
+    )(ms, acts, slopes, theirs, sums, begun)
     grads = lax.all_to_all(grads, "batch", 0, 0, tiled=True)
     total = call(total_kernel, shape((2, 9 * C * C // nb), F32), "v", "v", [], 0, 10**6, 10**6)(grads)
     return starts, total

time: 75.5 us -> 75 us (level)
  transfers between devices with their start and end apart: 3 -> 3, of which waited for: 2 -> 3; matrix products, arithmetic and copies ran while one was open for 0% -> 0% of each run, Pallas kernels for 4% -> 3%
where the time goes in v3:
time: 75 us; the launch traced here: 74.8 us
  blocking collectives  52.8 us (70%)
  Pallas kernels  13.4 us (18%)
  waiting for transfers between devices  6.4 us (9%)
  starting transfers between devices  1.48 us (2%)
    all_to_all x1, blocking collectives, shards(): lax.all_to_all(pairs, 'section', 0, 0, axis_index_groups=groups, tiled=True)  31.6 us
    all_to_all x1, blocking collectives, shards(): grads = lax.all_to_all(grads, 'batch', 0, 0, tiled=True)  21.2 us
    ppermute x1, waiting for transfers between devices, shards(): lax.ppermute(last, 'section', [(i, i - half) for i in range(half, section...  5.13 us
    pallas_call x1, Pallas kernels, shards(): call(lower_kernel, (image, image), 'vvvv', 'vv', [((C, N), F32), ((C, N),...  3.23 us
    pallas_call x1, Pallas kernels, shards(): call(upper_kernel, image16, 'v', 'v', [], 0, 10 ** 9, 2 * 10 ** 6)(packed)  2.62 us
    pallas_call x1, Pallas kernels, shards(): call(give_kernel, (shape((C, 2 * N + WIDE), BF16), shape((2, 3 * C, 3 * C...  2.17 us
    pallas_call x1, Pallas kernels, shards(): call(other_kernel, (shape((nb, 9 * (C // nb), 2 * C), BF16), shape((1, 2,...  1.76 us
  transfers between devices with their start and end apart: 3, of which 3 were waited for; matrix products, arithmetic and copies ran while one was open for 0% of the time, Pallas kernels for 3%

profile of v3, /device:TPU:32, one launch (start us, length us, event | category | flops | bytes accessed | tf_op | source)
XLA Modules:
  0.0 74.8 jit_solution(9803481174914686643)
XLA Ops:
  0.6 2.2 %shard_map.59 = (bf16[64,2688]{1,0:T(8,128)(2,1)S(1)}, bf16[2,192,192]{2,1,0:T(8,128)(2,1)S(1)}, bf16[2,64,1024]{2,1,0:T(8,128)(2,1)S(1)}, f32[64,1024]{1,0:T(8,128)S(1)}, f32[64,1024]{1,0:T(8,128)S(1)}) custom-call(bf16[2,2,64,1024]{3,2,1,0:T(8,128)(2,1)} %states.3, bf16[2,64,576]{2,1,0:T(8,128)(2,1)} %weights.1, f32[1,2,64,1024]{3,2,1,0:T(8,128)} %guess.1, ...), custom_call_target="tpu_custom_call" | custom-call | flops 300000000 | bytes 2000000 | tf_op jit(solution)/shard_map/pallas_call | solution.py:282
  2.8 0.1 collective-permute-start
  2.9 0.8 %shard_map.61.keep = bf16[64,2048]{1,0:T(8,128)(2,1)S(1)} custom-call(bf16[2,192,192]{2,1,0:T(8,128)(2,1)S(1)} %get-tuple-element.18.ms, bf16[2,64,1024]{2,1,0:T(8,128)(2,1)S(1)} %get-tuple-element.21.u, f32[64,1024]{1,0:T(8,128)S(1)} %get-tuple-element.22.g, f32[64,1024]{1,0:T(8,128)S(1)} %get-tuple-element.23.lc), custom_call_target="tpu_custom_call" | custom-call | flops 300000000 | bytes 1000000 | tf_op jit(solution)/shard_map/pallas_call | solution.py:289
  3.8 0.8 %collective-permute-done.got = bf16[64,2688]{1,0:T(8,128)(2,1)S(1)} collective-permute-done((bf16[64,2688]{1,0:T(8,128)(2,1)S(1)}, bf16[64,2688]{1,0:T(8,128)(2,1)S(1)}, u32[]{:S(2)}, u32[]{:S(2)}) %collective-permute-start) | collective-permute-done | bytes 344096 | tf_op jit(solution)/shard_map/ppermute | solution.py:288
  4.5 0.5 shard_map.62
  5.1 31.6 %all_to_all.10.packed = bf16[4,64,4224]{2,1,0:T(8,128)(2,1)S(1)} all-to-all(bf16[4,64,4224]{2,1,0:T(8,128)(2,1)S(1)} %get-tuple-element.25), channel_id=1, replica_groups={{0,32,64,96},{16,48,80,112},{128,160,192,224},{144,176,208,240},{1,33,6..., dimensions={0} | all-to-all | bytes 4325376 | tf_op jit(solution)/shard_map/all_to_all | solution.py:294
  36.7 0.0 copy-start
  36.7 0.0 copy-start.1
  36.7 2.6 %shard_map.63 = bf16[64,1024]{1,0:T(8,128)(2,1)S(1)} custom-call(bf16[4,64,4224]{2,1,0:T(8,128)(2,1)S(1)} %all_to_all.10.packed), custom_call_target="tpu_custom_call" | custom-call | flops 1000000000 | bytes 2000000 | tf_op jit(solution)/shard_map/pallas_call | solution.py:300
  39.3 1.3 %collective-permute-start.1 = (bf16[64,1024]{1,0:T(8,128)(2,1)S(1)}, bf16[64,1024]{1,0:T(8,128)(2,1)S(1)}, u32[]{:S(2)}, u32[]{:S(2)}) collective-permute-start(bf16[64,1024]{1,0:T(8,128)(2,1)S(1)} %shard_map.63), channel_id=1, source_target_pairs={{128,0},{144,16},{160,32},{176,48},{192,64},{208,80},{224,96},{240... | collective-permute-start | bytes 393224 | tf_op jit(solution)/shard_map/ppermute | solution.py:301
  40.6 0.0 copy-done
  40.6 0.0 copy-done.1
  40.6 0.4 shard_map.60
  41.0 5.1 %collective-permute-done.1.start = bf16[64,1024]{1,0:T(8,128)(2,1)S(1)} collective-permute-done((bf16[64,1024]{1,0:T(8,128)(2,1)S(1)}, bf16[64,1024]{1,0:T(8,128)(2,1)S(1)}, u32[]{:S(2)}, u32[]{:S(2)}) %collective-permute-start.1) | collective-permute-done | bytes 131104 | tf_op jit(solution)/shard_map/ppermute | solution.py:301
  46.2 3.2 %shard_map.64 = (f32[64,1024]{1,0:T(8,128)S(1)}, f32[64,1024]{1,0:T(8,128)S(1)}) custom-call(bf16[64,1024]{1,0:T(8,128)(2,1)S(1)} %collective-permute-done.1.start, bf16[4,64,4224]{2,1,0:T(8,128)(2,1)S(1)} %all_to_all.10.packed, bf16[64,1024]{1,0:T(8,128)(2,1)S(1)} %get-tuple-element.26.odd, f32[64,1024]{1,0:T(8,128)S(1)} %get-tuple-element.27.base), custom_call_target="tpu_custom_call" | custom-call | flops 1200000000 | bytes 2000000 | tf_op jit(solution)/shard_map/pallas_call | solution.py:302
  49.4 0.1 collective-permute-start.2
  49.5 1.0 %shard_map.65 = (f32[2,192,192]{2,1,0:T(8,128)S(1)}, f32[64,1024]{1,0:T(8,128)S(1)}) custom-call(bf16[2,192,192]{2,1,0:T(8,128)(2,1)S(1)} %get-tuple-element.18.ms, bf16[2,2,192,1024]{3,2,1,0:T(8,128)(2,1)S(1)} %get-tuple-element.19.acts, f32[2,2,64,1024]{3,2,1,0:T(8,128)S(1)} %get-tuple-element.20.slopes, f32[64,1024]{1,0:T(8,128)S(1)} %get-tuple-element.29.mine), custom_call_target="tpu_custom_call" | custom-call | flops 400000000 | bytes 1000000 | tf_op jit(solution)/shard_map/pallas_call | solution.py:308
  50.6 0.5 collective-permute-done.2.other
  51.0 1.8 %shard_map.66 = (bf16[16,36,128]{2,1,0:T(8,128)(2,1)S(1)}, f32[1,2,64,1024]{3,2,1,0:T(8,128)}) custom-call(bf16[2,192,192]{2,1,0:T(8,128)(2,1)S(1)} %get-tuple-element.18.ms, bf16[2,2,192,1024]{3,2,1,0:T(8,128)(2,1)S(1)} %get-tuple-element.19.acts, f32[2,2,64,1024]{3,2,1,0:T(8,128)S(1)} %get-tuple-element.20.slopes, ...), custom_call_target="tpu_custom_call" | custom-call | flops 400000000 | bytes 1000000 | tf_op jit(solution)/shard_map/pallas_call | solution.py:311
  52.8 21.2 %all_to_all.11.parts = bf16[16,36,128]{2,1,0:T(8,128)(2,1)S(1)} all-to-all(bf16[16,36,128]{2,1,0:T(8,128)(2,1)S(1)} %get-tuple-element.33), channel_id=1, replica_groups=mesh['section'=16,'batch'=16] {'batch'}, dimensions={0} | all-to-all | bytes 294912 | tf_op jit(solution)/shard_map/all_to_all | solution.py:315
  74.0 0.8 %shard_map.67 = f32[2,2304]{1,0:T(2,128)} custom-call(bf16[16,36,128]{2,1,0:T(8,128)(2,1)S(1)} %all_to_all.11.parts), custom_call_target="tpu_custom_call" | custom-call | flops 1000000 | bytes 1000000 | tf_op jit(solution)/shard_map/pallas_call | solution.py:316
Async XLA Ops:
  2.8 1.7 %collective-permute-start = (bf16[64,2688]{1,0:T(8,128)(2,1)S(1)}, bf16[64,2688]{1,0:T(8,128)(2,1)S(1)}, u32[]{:S(2)}, u32[]{:S(2)}) collective-permute-start(bf16[64,2688]{1,0:T(8,128)(2,1)S(1)} %get-tuple-element.24), channel_id=1, source_target_pairs={{0,16},{16,0},{32,48},{48,32},{64,80},{80,64},{96,112},{112,96},{1... | collective-permute-start | bytes 1032200 | tf_op jit(solution)/shard_map/ppermute | solution.py:288
  36.7 3.9 %copy-start = (bf16[2,2,64,1024]{3,2,1,0:T(8,128)(2,1)S(1)}, bf16[2,2,64,1024]{3,2,1,0:T(8,128)(2,1)}, u32[]{:S(2)}) copy-start(bf16[2,2,64,1024]{3,2,1,0:T(8,128)(2,1)} %states.3) | copy-start | bytes 1572868
  36.7 3.9 %copy-start.1 = (f32[2,64,1024]{2,1,0:T(8,128)S(1)}, f32[2,64,1024]{2,1,0:T(8,128)}, u32[]{:S(2)}) copy-start(f32[2,64,1024]{2,1,0:T(8,128)} %loss.3) | copy-start | bytes 1572868
  39.3 6.9 %collective-permute-start.1 = (bf16[64,1024]{1,0:T(8,128)(2,1)S(1)}, bf16[64,1024]{1,0:T(8,128)(2,1)S(1)}, u32[]{:S(2)}, u32[]{:S(2)}) collective-permute-start(bf16[64,1024]{1,0:T(8,128)(2,1)S(1)} %shard_map.63), channel_id=1, source_target_pairs={{128,0},{144,16},{160,32},{176,48},{192,64},{208,80},{224,96},{240... | collective-permute-start | bytes 393224 | tf_op jit(solution)/shard_map/ppermute | solution.py:301
  49.4 1.6 %collective-permute-start.2 = (f32[64,1024]{1,0:T(8,128)S(1)}, f32[64,1024]{1,0:T(8,128)S(1)}, u32[]{:S(2)}, u32[]{:S(2)}) collective-permute-start(f32[64,1024]{1,0:T(8,128)S(1)} %get-tuple-element.28), channel_id=1, source_target_pairs={{0,16},{16,0},{32,48},{48,32},{64,80},{80,64},{96,112},{112,96},{1... | collective-permute-start | bytes 786440 | tf_op jit(solution)/shard_map/ppermute | solution.py:306
